TPU v7x, 256 devices: a whole 4x4x8 slice. The times are simulated.
256 devices in a mesh: cam: 8 (over z), tm: 32 (over x, y, core).
Axes of the slice: x: 4, y: 4, z: 8, core: 2. Of those that a mesh axis runs over, the one named last changes fastest.
Arguments:
- embeds: bfloat16 [8, 4096, 2048], P(None, 'tm', 'cam'), may hold values from -6 to 6
- w_in: bfloat16 [2048, 2304], replicated, may hold values from -0.125 to 0.125
- log_decay: float32 [8, 32, 4096], P('cam', None, 'tm'), may hold values from -1 to 0, as said below
- clip_keep: float32 [32], replicated, may hold values from 0.55 to 0.8
- clip_starts: int32 [8, 3], P('cam'), may hold values from 1 to 4095
- valid_len: int32 [8], P('cam'), may hold values from 2048 to 4096, as said below
- norm_gain: float32 [2048], replicated, may hold values from 0.1 to 1.9
- g_out: bfloat16 [8, 4096, 2048], P('cam', 'tm'), may hold values from -6 to 6
Outputs:
- layer_out: bfloat16 [8, 4096, 2048], P('cam', 'tm')
- d_embeds: bfloat16 [8, 4096, 2048], P(None, 'tm', 'cam')
- d_w_in: float32 [2048, 2304], P(('cam', 'tm'))
Inputs may be any that keep to these rules, and one draw needn't show every extreme that they name: `log_decay`: negative. `valid_len`: some camera's valid length is 4096 in every draw.
All inputs are finite; a program needn't handle non-finite values.
Results may differ from a plain program's by a relative error of at most 0.014.
Values may be sent and summed in bfloat16 or wider, within the bound.
A program may use at most 128 MiB of HBM per device.

v0:
```python
import math
import jax
import jax.numpy as jnp
from jax import lax
from jax.sharding import PartitionSpec as P

D = 2048
H = 32
P_SIZE = 64
N = 128
Q = 128
HP = 2048
epsilon = 1e-05
precise = lax.Precision.HIGHEST


def prefix_states(block_log, state, reverse):
    size = lax.axis_size("tm")
    extra = jnp.broadcast_to(block_log[:, None, None], (H, 8, N))
    packed = jnp.concatenate([state, extra], axis=1)
    mine = lax.all_to_all(packed, "tm", split_axis=0, concat_axis=0, tiled=True)
    logs = mine[:, P_SIZE, 0]
    parts = mine[:, :P_SIZE].reshape(size, P_SIZE * N)
    cum = jnp.cumsum(logs)
    at = jnp.arange(size)
    if reverse:
        reach = at[None, :] > at[:, None]
        gap = (cum - logs)[None, :] - cum[:, None]
    else:
        reach = at[None, :] < at[:, None]
        gap = (cum - logs)[:, None] - cum[None, :]
    factors = jnp.where(reach, jnp.exp(jnp.where(reach, gap, 0.0)), 0.0)
    entered = jnp.dot(factors, parts, precision=precise).astype(jnp.bfloat16)
    entered = entered.reshape(size, P_SIZE, N)
    return lax.all_to_all(entered, "tm", split_axis=0, concat_axis=0, tiled=True).astype(
        jnp.float32
    )


def on_device(embeds, w_in, log_decay, clip_keep, clip_starts, valid_len, norm_gain, g_out):
    n_cam = lax.axis_size("cam")
    n_tm = lax.axis_size("tm")
    t_dev = embeds.shape[1]
    groups = t_dev // Q
    x_rows = lax.all_to_all(embeds, "cam", split_axis=0, concat_axis=2, tiled=True)[0]
    projected = jnp.dot(x_rows, w_in, preferred_element_type=jnp.float32).astype(jnp.bfloat16)
    positions = lax.axis_index("tm") * t_dev + jnp.arange(t_dev, dtype=jnp.int32)
    is_start = jnp.any(positions[:, None] == clip_starts[0][None, :], axis=1)
    log_rates = log_decay[0] + jnp.where(is_start[None, :], jnp.log(clip_keep)[:, None], 0.0)
    valid_rows = (positions < valid_len[0]).astype(jnp.float32)
    proj_float = projected.astype(jnp.float32)
    x_blocks = (proj_float[:, :HP].reshape(t_dev, H, P_SIZE) * valid_rows[:, None, None]).reshape(
        groups, Q, H, P_SIZE
    )
    b_blocks = proj_float[:, HP : HP + N].reshape(groups, Q, N)
    c_blocks = proj_float[:, HP + N :].reshape(groups, Q, N)
    cum_rate = jnp.cumsum(log_rates.reshape(H, groups, Q), axis=2).transpose(1, 0, 2)
    group_log = cum_rate[:, :, -1]
    causal = jnp.arange(Q)[:, None] >= jnp.arange(Q)[None, :]
    gaps = cum_rate[:, :, :, None] - cum_rate[:, :, None, :]
    weights = jnp.where(causal, jnp.exp(jnp.where(causal, gaps, 0.0)), 0.0)
    scores = jnp.einsum("ktn,ksn->kts", c_blocks, b_blocks, precision=precise)
    mixing = weights * scores[:, None]
    y_in = jnp.einsum("khts,kshp->kthp", mixing, x_blocks, precision=precise)
    tail_decay = jnp.exp(group_log[:, :, None] - cum_rate).transpose(0, 2, 1)
    lift_decay = jnp.exp(cum_rate).transpose(0, 2, 1)
    local_state = jnp.einsum(
        "kshp,ksn->khpn", x_blocks * tail_decay[:, :, :, None], b_blocks, precision=precise
    )
    zero_before = [jnp.zeros((H, P_SIZE, N), jnp.float32)]
    zero_end = jnp.exp(group_log[-1])[:, None, None] * zero_before[-1] + local_state[-1]
    block_log = jnp.sum(group_log, axis=0)
    s_in = prefix_states(block_log, zero_end, False)
    lead_log = jnp.cumsum(group_log, axis=0) - group_log
    state_before = jnp.exp(lead_log)[:, :, None, None] * s_in[None] + jnp.stack(zero_before)
    y_out = lift_decay[:, :, :, None] * jnp.einsum(
        "khpn,ktn->kthp", state_before, c_blocks, precision=precise
    )
    raw_out = (y_in + y_out).reshape(t_dev, H, P_SIZE)
    inv_rms = lax.rsqrt(jnp.mean(raw_out * raw_out, axis=-1, keepdims=True) + epsilon)
    normed = raw_out * inv_rms
    layer_out = (normed.reshape(t_dev, HP) * norm_gain[None, :] * valid_rows[:, None]).astype(
        jnp.bfloat16
    )
    d_normed = (g_out[0].astype(jnp.float32) * norm_gain[None, :] * valid_rows[:, None]).reshape(
        t_dev, H, P_SIZE
    )
    d_output = inv_rms * (d_normed - normed * jnp.mean(d_normed * normed, axis=-1, keepdims=True))
    d_blocks = d_output.reshape(groups, Q, H, P_SIZE)
    back_state = jnp.einsum(
        "kthp,ktn->khpn", d_blocks * lift_decay[:, :, :, None], c_blocks, precision=precise
    )
    zero_after = [jnp.zeros((H, P_SIZE, N), jnp.float32)]
    zero_start = jnp.exp(group_log[0])[:, None, None] * zero_after[0] + back_state[0]
    r_out = prefix_states(block_log, zero_start, True)
    trail_log = jnp.cumsum(group_log[::-1], axis=0)[::-1] - group_log
    grad_after = jnp.exp(trail_log)[:, :, None, None] * r_out[None] + jnp.stack(zero_after)
    d_inputs = jnp.einsum("khts,kthp->kshp", mixing, d_blocks, precision=precise)
    d_inputs = d_inputs + tail_decay[:, :, :, None] * jnp.einsum(
        "khpn,ksn->kshp", grad_after, b_blocks, precision=precise
    )
    pair_terms = weights * jnp.einsum("kthp,kshp->khts", d_blocks, x_blocks, precision=precise)
    d_c = jnp.einsum("khts,ksn->ktn", pair_terms, b_blocks, precision=precise)
    d_c = d_c + jnp.einsum(
        "kthp,khpn->ktn", d_blocks * lift_decay[:, :, :, None], state_before, precision=precise
    )
    d_b = jnp.einsum("khts,ktn->ksn", pair_terms, c_blocks, precision=precise)
    d_b = d_b + jnp.einsum(
        "kshp,khpn->ksn", x_blocks * tail_decay[:, :, :, None], grad_after, precision=precise
    )
    du_rows = d_inputs.reshape(t_dev, HP) * valid_rows[:, None]
    d_proj = jnp.concatenate(
        [du_rows, d_b.reshape(t_dev, N), d_c.reshape(t_dev, N)], axis=1
    ).astype(jnp.bfloat16)
    all_proj = lax.all_gather(d_proj, "cam").reshape(n_cam * t_dev, HP + 2 * N)
    width = D // n_cam
    w_mine = lax.dynamic_slice_in_dim(w_in, lax.axis_index("cam") * width, width, axis=0)
    d_embeds = (
        lax.dot_general(
            all_proj, w_mine, (((1,), (1,)), ((), ())), preferred_element_type=jnp.float32
        )
        .astype(jnp.bfloat16)
        .reshape(n_cam, t_dev, width)
    )
    grad_scale = 1.0 / math.sqrt(n_cam * t_dev * n_tm)
    row_terms = grad_scale * lax.dot_general(
        embeds.reshape(n_cam * t_dev, width),
        all_proj,
        (((0,), (0,)), ((), ())),
        preferred_element_type=jnp.float32,
    )
    d_w_in = lax.psum_scatter(row_terms, "tm", scatter_dimension=0, tiled=True)
    return (layer_out[None], d_embeds, d_w_in)


def solution(mesh):
    return jax.shard_map(
        on_device,
        mesh=mesh,
        in_specs=(
            P(None, "tm", "cam"),
            P(),
            P("cam", None, "tm"),
            P(),
            P("cam", None),
            P("cam"),
            P(),
            P("cam", "tm", None),
        ),
        out_specs=(P("cam", "tm", None), P(None, "tm", "cam"), P(("cam", "tm"), None)),
        check_vma=False,
    )
```

profile of v0, /device:TPU:2, one launch (start us, length us, event | category | flops | bytes accessed | tf_op | source)
XLA Modules:
  0.0 300.5 jit_solution(2047633472301824590)
XLA Ops:
  7.2 2.1 copy.62
  9.3 8.5 %all-to-all-start = ((bf16[8,128,256]{1,2,0:T(8,128)(2,1)}), bf16[8,128,256]{1,2,0:T(8,128)(2,1)S(1)}, u32[]{:S(2)}, u32[]{:S(2)}) async-start(bf16[8,128,256]{1,2,0:T(8,128)(2,1)} %copy.62), calls=%async_computation | async-start | bytes 1048576 | tf_op jit(solution)/shard_map/all_to_all | solution.py:45
  19.6 15.6 %all-to-all-done = bf16[8,128,256]{1,2,0:T(8,128)(2,1)S(1)} async-done(((bf16[8,128,256]{1,2,0:T(8,128)(2,1)}), bf16[8,128,256]{1,2,0:T(8,128)(2,1)S(1)}, u32[]{:S(2)}, u32[]{:S(2)}) %all-to-all-start) | async-done | bytes 524320 | tf_op jit(solution)/shard_map/all_to_all | solution.py:45
  35.2 5.1 %convolution_convert_fusion.2 = bf16[128,2304]{1,0:T(8,128)(2,1)S(1)} fusion(bf16[128,2048]{0,1:T(8,128)(2,1)S(1)} %bitcast.133, bf16[2048,2304]{1,0:T(8,128)(2,1)} %param.9), kind=kOutput, calls=%fused_computation.5 | convolution fusion | flops 1208254464 | bytes 10551296 | tf_op jit(solution)/shard_map/dot_general | solution.py:46
  42.7 7.8 %all-to-all-start.1 = ((f32[32,72,128]{2,1,0:T(8,128)}), f32[32,72,128]{2,1,0:T(8,128)}, u32[]{:S(2)}, u32[]{:S(2)}) async-start(f32[32,72,128]{2,1,0:T(8,128)} %pad_maximum_fusion.1), calls=%async_computation.1 | async-start | bytes 2359296 | tf_op jit(solution)/shard_map/all_to_all | solution.py:21
  51.9 14.5 %all-to-all-done.1 = f32[32,72,128]{2,1,0:T(8,128)} async-done(((f32[32,72,128]{2,1,0:T(8,128)}), f32[32,72,128]{2,1,0:T(8,128)}, u32[]{:S(2)}, u32[]{:S(2)}) %all-to-all-start.1) | async-done | bytes 1179680 | tf_op jit(solution)/shard_map/all_to_all | solution.py:21
  71.6 6.9 %all-to-all-start.2 = ((bf16[32,64,128]{2,1,0:T(8,128)(2,1)}), bf16[32,64,128]{2,1,0:T(8,128)(2,1)}, u32[]{:S(2)}, u32[]{:S(2)}) async-start(bf16[32,64,128]{2,1,0:T(8,128)(2,1)} %bitcast.135), calls=%async_computation.2 | async-start | bytes 1048576 | tf_op jit(solution)/shard_map/all_to_all | solution.py:35
  79.6 2.6 copy.63
  82.3 6.5 %fusion.7 = f32[1,128,32,64]{1,3,2,0:T(8,128)} fusion(f32[128,128]{1,0:T(8,128)S(1)} %fusion.65, f32[32,128]{1,0:T(8,128)S(1)} %bitcast.139, pred[128,128]{1,0:T(8,128)(4,1)S(1)} %iota_compare_fusion, f32[128,32,64]{0,2,1:T(8,128)} %bitcast.136, f32[128]{0:T(128)S(1)} %compare_convert_fusion), kind=kOutput, calls=%fused_computation.13 | convolution fusion | flops 405012480 | bytes 2195968 | tf_op jit(solution)/shard_map/khts,kshp->kthp/dot_general | solution.py:64
  88.8 2.2 fusion.32
  95.6 7.5 %all-to-all-start.3 = ((f32[32,72,128]{2,1,0:T(8,128)}), f32[32,72,128]{2,1,0:T(8,128)}, u32[]{:S(2)}, u32[]{:S(2)}) async-start(f32[32,72,128]{2,1,0:T(8,128)} %pad_maximum_fusion), calls=%async_computation.3 | async-start | bytes 2359296 | tf_op jit(solution)/shard_map/all_to_all | solution.py:21
  103.1 5.2 %multiply_reduce_fusion = f32[128,128]{1,0:T(8,128)S(1)} fusion(f32[1,128,32,64]{1,3,2,0:T(8,128)S(1)} %subtract_multiply_fusion, f32[32,128]{1,0:T(8,128)S(1)} %bitcast.140, pred[128,128]{1,0:T(8,128)(4,1)S(1)} %iota_compare_fusion, f32[128,32,64]{0,2,1:T(8,128)} %bitcast.137, f32[128]{0:T(128)S(1)} %compare_convert_fusion), kind=kOutput, calls=%fused_computation.6 | convolution fusion | flops 405520384 | bytes 2195968 | tf_op jit(solution)/shard_map/kthp,kshp->khts/dot_general | solution.py:102
  108.3 10.7 %all-to-all-done.3 = f32[32,72,128]{2,1,0:T(8,128)} async-done(((f32[32,72,128]{2,1,0:T(8,128)}), f32[32,72,128]{2,1,0:T(8,128)}, u32[]{:S(2)}, u32[]{:S(2)}) %all-to-all-start.3) | async-done | bytes 1179680 | tf_op jit(solution)/shard_map/all_to_all | solution.py:21
  124.2 7.1 %all-to-all-start.4 = ((bf16[32,64,128]{2,1,0:T(8,128)(2,1)}), bf16[32,64,128]{2,1,0:T(8,128)(2,1)}, u32[]{:S(2)}, u32[]{:S(2)}) async-start(bf16[32,64,128]{2,1,0:T(8,128)(2,1)} %bitcast.134), calls=%async_computation.4 | async-start | bytes 1048576 | tf_op jit(solution)/shard_map/all_to_all | solution.py:35
  131.4 3.0 convolution_bitcast_fusion.1
  135.3 3.4 %fusion.10 = f32[1,128,32,64]{1,3,2,0:T(8,128)} fusion(f32[1,128,32,64]{1,3,2,0:T(8,128)S(1)} %subtract_multiply_fusion, f32[128,128]{1,0:T(8,128)S(1)} %fusion.65, f32[32,128]{1,0:T(8,128)S(1)} %bitcast.141, pred[128,128]{1,0:T(8,128)(4,1)S(1)} %iota_compare_fusion), kind=kOutput, calls=%fused_computation.14 | convolution fusion | flops 404750336 | bytes 2195456 | tf_op jit(solution)/shard_map/khts,kthp->kshp/dot_general | solution.py:98
  138.7 2.6 all-to-all-done.4
  141.3 2.9 convolution_bitcast_fusion.2
  145.2 1.8 fusion.16
  148.4 53.9 %all-gather.2.cloned.1.call-done = bf16[8,128,2304]{2,1,0:T(8,128)(2,1)} async-done(((bf16[1,128,2304]{2,1,0:T(8,128)(2,1)}), bf16[8,128,2304]{2,1,0:T(8,128)(2,1)}) %all-gather.2.cloned.1.call-update) | async-done | bytes 4718608 | tf_op jit(solution)/shard_map/all_gather | solution.py:115
  202.3 3.9 %fusion.1 = f32[256,2304]{0,1:T(8,128)S(1)} fusion(bf16[8,128,2304]{2,1,0:T(8,128)(2,1)} %all-gather.2.cloned.1.call-done, bf16[8,128,256]{2,1,0:T(8,128)(2,1)} %param.8), kind=kOutput, calls=%fused_computation.4 | convolution fusion | flops 1208549376 | bytes 7602176 | tf_op jit(solution)/shard_map/dot_general | solution.py:126
  206.2 2.0 copy.86
  209.9 4.9 %convolution_convert_fusion.3 = bf16[1024,256]{1,0:T(8,128)(2,1)} fusion(bf16[1024,2304]{1,0:T(8,128)(2,1)} %bitcast.144, bf16[2048,2304]{1,0:T(8,128)(2,1)} %param.9, s32[]{:T(128)S(6)} %select_n.49), kind=kOutput, calls=%fused_computation.23 | convolution fusion | flops 1208221696 | bytes 6422532 | tf_op jit(solution)/shard_map/dot_general | solution.py:119
  214.8 78.9 %reduce-scatter.4.cloned.1.call-done = f32[8,2304]{1,0:T(8,128)} async-done(((f32[256,2304]{1,0:T(8,128)}), f32[8,2304]{1,0:T(8,128)}) %reduce-scatter.4.cloned.1.call-update) | async-done | bytes 73744
  (69 shorter events, 26.2 us)
Async XLA Ops:
  7.2 10.6 %copy-start.5 = (s32[1,3]{1,0:T(1,128)S(1)}, s32[1,3]{1,0:T(1,128)}, u32[]{:S(2)}) copy-start(s32[1,3]{1,0:T(1,128)} %param.12) | copy-start | bytes 40
  7.2 10.6 %copy-start.6 = (f32[32]{0:T(128)S(1)}, f32[32]{0:T(128)}, u32[]{:S(2)}) copy-start(f32[32]{0:T(128)} %param.11) | copy-start | bytes 388
  7.2 11.3 %copy-start.4 = (f32[1,32,128]{2,1,0:T(8,128)S(1)}, f32[1,32,128]{2,1,0:T(8,128)}, u32[]{:S(2)}) copy-start(f32[1,32,128]{2,1,0:T(8,128)} %param.10) | copy-start | bytes 49156
  9.3 26.0 %all-to-all-start = ((bf16[8,128,256]{1,2,0:T(8,128)(2,1)}), bf16[8,128,256]{1,2,0:T(8,128)(2,1)S(1)}, u32[]{:S(2)}, u32[]{:S(2)}) async-start(bf16[8,128,256]{1,2,0:T(8,128)(2,1)} %copy.62), calls=%async_computation | async-start | bytes 1048576 | tf_op jit(solution)/shard_map/all_to_all | solution.py:45
  40.3 41.9 %copy-start.1 = (bf16[128,2304]{1,0:T(8,128)(2,1)}, bf16[128,2304]{1,0:T(8,128)(2,1)S(1)}, u32[]{:S(2)}) copy-start(bf16[128,2304]{1,0:T(8,128)(2,1)S(1)} %convolution_convert_fusion.2) | copy-start | bytes 1769476
  42.7 9.1 %copy-start.3 = (f32[2048]{0:T(1024)S(1)}, f32[2048]{0:T(1024)}, u32[]{:S(2)}) copy-start(f32[2048]{0:T(1024)} %param.14) | copy-start | bytes 24580
  42.7 23.7 %all-to-all-start.1 = ((f32[32,72,128]{2,1,0:T(8,128)}), f32[32,72,128]{2,1,0:T(8,128)}, u32[]{:S(2)}, u32[]{:S(2)}) async-start(f32[32,72,128]{2,1,0:T(8,128)} %pad_maximum_fusion.1), calls=%async_computation.1 | async-start | bytes 2359296 | tf_op jit(solution)/shard_map/all_to_all | solution.py:21
  51.8 39.3 %copy-start = (f32[1,128,2048]{1,2,0:T(8,128)}, f32[1,128,2048]{1,2,0:T(8,128)S(1)}, u32[]{:S(2)}) copy-start(f32[1,128,2048]{1,2,0:T(8,128)S(1)} %copy.69) | copy-start | bytes 3145732
  71.6 17.2 %all-to-all-start.2 = ((bf16[32,64,128]{2,1,0:T(8,128)(2,1)}), bf16[32,64,128]{2,1,0:T(8,128)(2,1)}, u32[]{:S(2)}, u32[]{:S(2)}) async-start(bf16[32,64,128]{2,1,0:T(8,128)(2,1)} %bitcast.135), calls=%async_computation.2 | async-start | bytes 1048576 | tf_op jit(solution)/shard_map/all_to_all | solution.py:35
  95.6 23.4 %all-to-all-start.3 = ((f32[32,72,128]{2,1,0:T(8,128)}), f32[32,72,128]{2,1,0:T(8,128)}, u32[]{:S(2)}, u32[]{:S(2)}) async-start(f32[32,72,128]{2,1,0:T(8,128)} %pad_maximum_fusion), calls=%async_computation.3 | async-start | bytes 2359296 | tf_op jit(solution)/shard_map/all_to_all | solution.py:21
  124.2 17.0 %all-to-all-start.4 = ((bf16[32,64,128]{2,1,0:T(8,128)(2,1)}), bf16[32,64,128]{2,1,0:T(8,128)(2,1)}, u32[]{:S(2)}, u32[]{:S(2)}) async-start(bf16[32,64,128]{2,1,0:T(8,128)(2,1)} %bitcast.134), calls=%async_computation.4 | async-start | bytes 1048576 | tf_op jit(solution)/shard_map/all_to_all | solution.py:35
  131.4 70.9 %all-gather.2.cloned.1.call-start = ((), (), s32[]{:S(2)}) async-start(), calls=%async_computation.6 | async-start | bytes 5308416 | tf_op jit(solution)/shard_map/all_gather | solution.py:115
  138.7 6.5 %copy-start.2 = (f32[1,128,32,64]{1,3,2,0:T(8,128)S(1)}, f32[1,128,32,64]{1,3,2,0:T(8,128)}, u32[]{:S(2)}) copy-start(f32[1,128,32,64]{1,3,2,0:T(8,128)} %fusion.10) | copy-start | bytes 3145732
  148.4 145.3 %reduce-scatter.4.cloned.1.call-start = ((), (), s32[]{:S(2)}) async-start(), calls=%async_computation.7 | async-start | bytes 2433024
Sparse Core Ops, SparseCore 0:
  148.5 53.7 all-gather.1
  208.4 85.3 reduce-scatter.3
where the time goes:
time: 302 us; the launch traced here: 301 us
  waiting for transfers between devices  176 us (58%)
  matrix products  46 us (15%)
  starting transfers between devices  37.9 us (13%)
  local copies, waits for them, and re-layouts  17 us (6%)
  between operations  15.1 us (5%)
  other arithmetic  8.47 us (3%)
    unnamed x3, waiting for transfers between devices  78.9 us
    all_gather x1, waiting for transfers between devices, on_device(): all_proj = lax.all_gather(d_proj, 'cam').reshape(n_cam * t_dev, HP + 2 * N)  53.9 us
    all_to_all x2, waiting for transfers between devices, prefix_states(): mine = lax.all_to_all(packed, 'tm', split_axis=0, concat_axis=0, tiled=True)  25.2 us
    all_to_all x1, waiting for transfers between devices, on_device(): lax.all_to_all(embeds, 'cam', split_axis=0, concat_axis=2, tiled=True)[0]  15.6 us
    all_to_all x2, starting transfers between devices, prefix_states(): mine = lax.all_to_all(packed, 'tm', split_axis=0, concat_axis=0, tiled=True)  15.3 us
    all_to_all x2, starting transfers between devices, prefix_states(): lax.all_to_all(entered, 'tm', split_axis=0, concat_axis=0, tiled=True)  14 us
    all_to_all x1, starting transfers between devices, on_device(): lax.all_to_all(embeds, 'cam', split_axis=0, concat_axis=2, tiled=True)[0]  8.47 us
    dot_general x1, matrix products, on_device(): y_in = jnp.einsum('khts,kshp->kthp', mixing, x_blocks, precision=precise)  6.51 us
  transfers between devices with their start and end apart: 7, of which 6 were waited for; matrix products, arithmetic and copies ran while one was open for 11% of the time, Pallas kernels for 0%

commit v1 on v0

--- a/solution.py
+++ b/solution.py
@@ -12,6 +12,13 @@
 HP = 2048
 epsilon = 1e-05
 precise = lax.Precision.HIGHEST
+
+
+def trade_parts(shard, axis, split, join):
+    size = lax.axis_size(axis)
+    shards = jnp.stack(jnp.split(shard, size, axis=split), axis=0)
+    shards = lax.all_to_all(shards, axis, split_axis=0, concat_axis=0)
+    return jnp.concatenate(shards, axis=join)
 
 
 def prefix_states(block_log, state, reverse):
@@ -42,7 +49,7 @@
     n_tm = lax.axis_size("tm")
     t_dev = embeds.shape[1]
     groups = t_dev // Q
-    x_rows = lax.all_to_all(embeds, "cam", split_axis=0, concat_axis=2, tiled=True)[0]
+    x_rows = trade_parts(embeds, "cam", 0, 2)[0]
     projected = jnp.dot(x_rows, w_in, preferred_element_type=jnp.float32).astype(jnp.bfloat16)
     positions = lax.axis_index("tm") * t_dev + jnp.arange(t_dev, dtype=jnp.int32)
     is_start = jnp.any(positions[:, None] == clip_starts[0][None, :], axis=1)

time: 302 us -> 307 us (1.017)
  local copies, waits for them, and re-layouts: 17 us -> 22 us
    unnamed x18 -> x32, local copies, waits for them, and re-layouts: 5.9 us -> 9.21 us
  transfers between devices with their start and end apart: 7 -> 7, of which waited for: 6 -> 6; matrix products, arithmetic and copies ran while one was open for 11% -> 10% of each run, Pallas kernels for 0% -> 0%
where the time goes in v1:
time: 307 us; the launch traced here: 306 us
  waiting for transfers between devices  176 us (57%)
  matrix products  46 us (15%)
  starting transfers between devices  37.9 us (12%)
  local copies, waits for them, and re-layouts  22 us (7%)
  between operations  15.1 us (5%)
  other arithmetic  8.47 us (3%)
    unnamed x3, waiting for transfers between devices  78.9 us
    all_gather x1, waiting for transfers between devices, on_device(): all_proj = lax.all_gather(d_proj, 'cam').reshape(n_cam * t_dev, HP + 2 * N)  53.9 us
    all_to_all x2, waiting for transfers between devices, prefix_states(): mine = lax.all_to_all(packed, 'tm', split_axis=0, concat_axis=0, tiled=True)  25.2 us
    all_to_all x1, waiting for transfers between devices, trade_parts(): shards = lax.all_to_all(shards, axis, split_axis=0, concat_axis=0)  15.6 us
    all_to_all x2, starting transfers between devices, prefix_states(): mine = lax.all_to_all(packed, 'tm', split_axis=0, concat_axis=0, tiled=True)  15.3 us
    all_to_all x2, starting transfers between devices, prefix_states(): lax.all_to_all(entered, 'tm', split_axis=0, concat_axis=0, tiled=True)  14 us
    unnamed x32, local copies, waits for them, and re-layouts  9.21 us
    all_to_all x1, starting transfers between devices, trade_parts(): shards = lax.all_to_all(shards, axis, split_axis=0, concat_axis=0)  8.47 us
  transfers between devices with their start and end apart: 7, of which 6 were waited for; matrix products, arithmetic and copies ran while one was open for 10% of the time, Pallas kernels for 0%

profile of v1, /device:TPU:2, one launch (start us, length us, event | category | flops | bytes accessed | tf_op | source)
XLA Modules:
  0.0 305.7 jit_solution(15883910910922309794)
XLA Ops:
  14.4 8.5 %all-to-all-start = ((bf16[8,1,128,256]{2,3,1,0:T(8,128)(2,1)}), bf16[8,1,128,256]{2,3,1,0:T(8,128)(2,1)S(1)}, u32[]{:S(2)}, u32[]{:S(2)}) async-start(bf16[8,1,128,256]{2,3,1,0:T(8,128)(2,1)} %bitcast_dynamic-update-slice_fusion), calls=%async_computation | async-start | bytes 1048576 | tf_op jit(solution)/shard_map/all_to_all | solution.py:20
  24.7 15.6 %all-to-all-done = bf16[8,1,128,256]{2,3,1,0:T(8,128)(2,1)S(1)} async-done(((bf16[8,1,128,256]{2,3,1,0:T(8,128)(2,1)}), bf16[8,1,128,256]{2,3,1,0:T(8,128)(2,1)S(1)}, u32[]{:S(2)}, u32[]{:S(2)}) %all-to-all-start) | async-done | bytes 524320 | tf_op jit(solution)/shard_map/all_to_all | solution.py:20
  40.3 5.1 %convolution_convert_fusion.2 = bf16[128,2304]{1,0:T(8,128)(2,1)S(1)} fusion(bf16[128,2048]{0,1:T(8,128)(2,1)S(1)} %bitcast.149, bf16[2048,2304]{1,0:T(8,128)(2,1)} %param.9), kind=kOutput, calls=%fused_computation.5 | convolution fusion | flops 1208254464 | bytes 10551296 | tf_op jit(solution)/shard_map/dot_general | solution.py:53
  47.8 7.8 %all-to-all-start.1 = ((f32[32,72,128]{2,1,0:T(8,128)}), f32[32,72,128]{2,1,0:T(8,128)}, u32[]{:S(2)}, u32[]{:S(2)}) async-start(f32[32,72,128]{2,1,0:T(8,128)} %pad_maximum_fusion.1), calls=%async_computation.1 | async-start | bytes 2359296 | tf_op jit(solution)/shard_map/all_to_all | solution.py:28
  57.0 14.5 %all-to-all-done.1 = f32[32,72,128]{2,1,0:T(8,128)} async-done(((f32[32,72,128]{2,1,0:T(8,128)}), f32[32,72,128]{2,1,0:T(8,128)}, u32[]{:S(2)}, u32[]{:S(2)}) %all-to-all-start.1) | async-done | bytes 1179680 | tf_op jit(solution)/shard_map/all_to_all | solution.py:28
  74.2 1.6 fusion.17
  76.7 6.9 %all-to-all-start.2 = ((bf16[32,64,128]{2,1,0:T(8,128)(2,1)}), bf16[32,64,128]{2,1,0:T(8,128)(2,1)}, u32[]{:S(2)}, u32[]{:S(2)}) async-start(bf16[32,64,128]{2,1,0:T(8,128)(2,1)} %bitcast.151), calls=%async_computation.2 | async-start | bytes 1048576 | tf_op jit(solution)/shard_map/all_to_all | solution.py:42
  84.8 2.6 copy.86
  87.4 6.5 %fusion.7 = f32[1,128,32,64]{1,3,2,0:T(8,128)} fusion(f32[128,128]{1,0:T(8,128)S(1)} %fusion.65, f32[32,128]{1,0:T(8,128)S(1)} %bitcast.155, pred[128,128]{1,0:T(8,128)(4,1)S(1)} %iota_compare_fusion, f32[128,32,64]{0,2,1:T(8,128)} %bitcast.152, f32[128]{0:T(128)S(1)} %compare_convert_fusion), kind=kOutput, calls=%fused_computation.13 | convolution fusion | flops 405012480 | bytes 2195968 | tf_op jit(solution)/shard_map/khts,kshp->kthp/dot_general | solution.py:71
  94.0 2.2 fusion.32
  100.7 7.5 %all-to-all-start.3 = ((f32[32,72,128]{2,1,0:T(8,128)}), f32[32,72,128]{2,1,0:T(8,128)}, u32[]{:S(2)}, u32[]{:S(2)}) async-start(f32[32,72,128]{2,1,0:T(8,128)} %pad_maximum_fusion), calls=%async_computation.3 | async-start | bytes 2359296 | tf_op jit(solution)/shard_map/all_to_all | solution.py:28
  108.2 5.2 %multiply_reduce_fusion = f32[128,128]{1,0:T(8,128)S(1)} fusion(f32[1,128,32,64]{1,3,2,0:T(8,128)S(1)} %subtract_multiply_fusion, f32[32,128]{1,0:T(8,128)S(1)} %bitcast.156, pred[128,128]{1,0:T(8,128)(4,1)S(1)} %iota_compare_fusion, f32[128,32,64]{0,2,1:T(8,128)} %bitcast.153, f32[128]{0:T(128)S(1)} %compare_convert_fusion), kind=kOutput, calls=%fused_computation.6 | convolution fusion | flops 405520384 | bytes 2195968 | tf_op jit(solution)/shard_map/kthp,kshp->khts/dot_general | solution.py:109
  113.4 10.7 %all-to-all-done.3 = f32[32,72,128]{2,1,0:T(8,128)} async-done(((f32[32,72,128]{2,1,0:T(8,128)}), f32[32,72,128]{2,1,0:T(8,128)}, u32[]{:S(2)}, u32[]{:S(2)}) %all-to-all-start.3) | async-done | bytes 1179680 | tf_op jit(solution)/shard_map/all_to_all | solution.py:28
  129.4 7.1 %all-to-all-start.4 = ((bf16[32,64,128]{2,1,0:T(8,128)(2,1)}), bf16[32,64,128]{2,1,0:T(8,128)(2,1)}, u32[]{:S(2)}, u32[]{:S(2)}) async-start(bf16[32,64,128]{2,1,0:T(8,128)(2,1)} %bitcast.150), calls=%async_computation.4 | async-start | bytes 1048576 | tf_op jit(solution)/shard_map/all_to_all | solution.py:42
  136.5 3.0 convolution_bitcast_fusion.1
  140.5 3.4 %fusion.10 = f32[1,128,32,64]{1,3,2,0:T(8,128)} fusion(f32[1,128,32,64]{1,3,2,0:T(8,128)S(1)} %subtract_multiply_fusion, f32[128,128]{1,0:T(8,128)S(1)} %fusion.65, f32[32,128]{1,0:T(8,128)S(1)} %bitcast.157, pred[128,128]{1,0:T(8,128)(4,1)S(1)} %iota_compare_fusion), kind=kOutput, calls=%fused_computation.14 | convolution fusion | flops 404750336 | bytes 2195456 | tf_op jit(solution)/shard_map/khts,kthp->kshp/dot_general | solution.py:105
  143.8 2.6 all-to-all-done.4
  146.4 2.9 convolution_bitcast_fusion.2
  150.4 1.8 fusion.16
  153.6 53.9 %all-gather.2.cloned.1.call-done = bf16[8,128,2304]{2,1,0:T(8,128)(2,1)} async-done(((bf16[1,128,2304]{2,1,0:T(8,128)(2,1)}), bf16[8,128,2304]{2,1,0:T(8,128)(2,1)}) %all-gather.2.cloned.1.call-update) | async-done | bytes 4718608 | tf_op jit(solution)/shard_map/all_gather | solution.py:122
  207.4 3.9 %fusion.1 = f32[256,2304]{0,1:T(8,128)S(1)} fusion(bf16[8,128,2304]{2,1,0:T(8,128)(2,1)} %all-gather.2.cloned.1.call-done, bf16[8,128,256]{2,1,0:T(8,128)(2,1)} %param.8), kind=kOutput, calls=%fused_computation.4 | convolution fusion | flops 1208549376 | bytes 7602176 | tf_op jit(solution)/shard_map/dot_general | solution.py:133
  211.3 2.0 copy.109
  215.1 4.9 %convolution_convert_fusion.3 = bf16[1024,256]{1,0:T(8,128)(2,1)} fusion(bf16[1024,2304]{1,0:T(8,128)(2,1)} %bitcast.160, bf16[2048,2304]{1,0:T(8,128)(2,1)} %param.9, s32[]{:T(128)S(6)} %select_n.49), kind=kOutput, calls=%fused_computation.23 | convolution fusion | flops 1208221696 | bytes 6422532 | tf_op jit(solution)/shard_map/dot_general | solution.py:126
  219.9 78.9 %reduce-scatter.4.cloned.1.call-done = f32[8,2304]{1,0:T(8,128)} async-done(((f32[256,2304]{1,0:T(8,128)}), f32[8,2304]{1,0:T(8,128)}) %reduce-scatter.4.cloned.1.call-update) | async-done | bytes 73744
  (85 shorter events, 31.7 us)
Async XLA Ops:
  7.2 15.7 %copy-start.5 = (s32[1,3]{1,0:T(1,128)S(1)}, s32[1,3]{1,0:T(1,128)}, u32[]{:S(2)}) copy-start(s32[1,3]{1,0:T(1,128)} %param.12) | copy-start | bytes 40
  7.2 15.8 %copy-start.6 = (f32[32]{0:T(128)S(1)}, f32[32]{0:T(128)}, u32[]{:S(2)}) copy-start(f32[32]{0:T(128)} %param.11) | copy-start | bytes 388
  7.2 16.4 %copy-start.4 = (f32[1,32,128]{2,1,0:T(8,128)S(1)}, f32[1,32,128]{2,1,0:T(8,128)}, u32[]{:S(2)}) copy-start(f32[1,32,128]{2,1,0:T(8,128)} %param.10) | copy-start | bytes 49156
  14.4 26.0 %all-to-all-start = ((bf16[8,1,128,256]{2,3,1,0:T(8,128)(2,1)}), bf16[8,1,128,256]{2,3,1,0:T(8,128)(2,1)S(1)}, u32[]{:S(2)}, u32[]{:S(2)}) async-start(bf16[8,1,128,256]{2,3,1,0:T(8,128)(2,1)} %bitcast_dynamic-update-slice_fusion), calls=%async_computation | async-start | bytes 1048576 | tf_op jit(solution)/shard_map/all_to_all | solution.py:20
  45.4 41.9 %copy-start.1 = (bf16[128,2304]{1,0:T(8,128)(2,1)}, bf16[128,2304]{1,0:T(8,128)(2,1)S(1)}, u32[]{:S(2)}) copy-start(bf16[128,2304]{1,0:T(8,128)(2,1)S(1)} %convolution_convert_fusion.2) | copy-start | bytes 1769476
  47.8 9.1 %copy-start.3 = (f32[2048]{0:T(1024)S(1)}, f32[2048]{0:T(1024)}, u32[]{:S(2)}) copy-start(f32[2048]{0:T(1024)} %param.14) | copy-start | bytes 24580
  47.8 23.7 %all-to-all-start.1 = ((f32[32,72,128]{2,1,0:T(8,128)}), f32[32,72,128]{2,1,0:T(8,128)}, u32[]{:S(2)}, u32[]{:S(2)}) async-start(f32[32,72,128]{2,1,0:T(8,128)} %pad_maximum_fusion.1), calls=%async_computation.1 | async-start | bytes 2359296 | tf_op jit(solution)/shard_map/all_to_all | solution.py:28
  56.9 39.3 %copy-start = (f32[1,128,2048]{1,2,0:T(8,128)}, f32[1,128,2048]{1,2,0:T(8,128)S(1)}, u32[]{:S(2)}) copy-start(f32[1,128,2048]{1,2,0:T(8,128)S(1)} %copy.92) | copy-start | bytes 3145732
  76.7 17.2 %all-to-all-start.2 = ((bf16[32,64,128]{2,1,0:T(8,128)(2,1)}), bf16[32,64,128]{2,1,0:T(8,128)(2,1)}, u32[]{:S(2)}, u32[]{:S(2)}) async-start(bf16[32,64,128]{2,1,0:T(8,128)(2,1)} %bitcast.151), calls=%async_computation.2 | async-start | bytes 1048576 | tf_op jit(solution)/shard_map/all_to_all | solution.py:42
  100.7 23.4 %all-to-all-start.3 = ((f32[32,72,128]{2,1,0:T(8,128)}), f32[32,72,128]{2,1,0:T(8,128)}, u32[]{:S(2)}, u32[]{:S(2)}) async-start(f32[32,72,128]{2,1,0:T(8,128)} %pad_maximum_fusion), calls=%async_computation.3 | async-start | bytes 2359296 | tf_op jit(solution)/shard_map/all_to_all | solution.py:28
  129.4 17.0 %all-to-all-start.4 = ((bf16[32,64,128]{2,1,0:T(8,128)(2,1)}), bf16[32,64,128]{2,1,0:T(8,128)(2,1)}, u32[]{:S(2)}, u32[]{:S(2)}) async-start(bf16[32,64,128]{2,1,0:T(8,128)(2,1)} %bitcast.150), calls=%async_computation.4 | async-start | bytes 1048576 | tf_op jit(solution)/shard_map/all_to_all | solution.py:42
  136.5 70.9 %all-gather.2.cloned.1.call-start = ((), (), s32[]{:S(2)}) async-start(), calls=%async_computation.6 | async-start | bytes 5308416 | tf_op jit(solution)/shard_map/all_gather | solution.py:122
  143.8 6.5 %copy-start.2 = (f32[1,128,32,64]{1,3,2,0:T(8,128)S(1)}, f32[1,128,32,64]{1,3,2,0:T(8,128)}, u32[]{:S(2)}) copy-start(f32[1,128,32,64]{1,3,2,0:T(8,128)} %fusion.10) | copy-start | bytes 3145732
  153.5 145.3 %reduce-scatter.4.cloned.1.call-start = ((), (), s32[]{:S(2)}) async-start(), calls=%async_computation.7 | async-start | bytes 2433024
Sparse Core Ops, SparseCore 0:
  153.6 53.7 all-gather.1
  213.5 85.3 reduce-scatter.3
